TPU v7x, 32 devices: a whole 2x2x4 slice. The times are simulated.
32 devices in a mesh: groups: 2 (over y), seq: 8 (over z, x), track: 2 (over core).
Axes of the slice: x: 2, y: 2, z: 4, core: 2. Of those that a mesh axis runs over, the one named last changes fastest.
Arguments:
- section_input: bfloat16 [1536, 4096], P('track', ('groups', 'seq')), parts along dimension 1, may hold values from -6 to 6
- conv_taps: float32 [1536, 3], P(('track', 'seq')), may hold values from -3 to 3
- dilation_level: int32 [1536], P(('track', 'seq')), may hold values from 0 to 4, as said below
- pointwise_matrix: bfloat16 [1536, 1536], P('track', 'seq'), may hold values from -0.15625 to 0.15625
- head_weight: bfloat16 [1536, 5312], P('seq', 'track'), may hold values from -0.078125 to 0.078125
- pred_error: bfloat16 [4096, 5312], P(('groups', 'seq'), 'track'), parts along dimension 0, may hold values from -6 to 6
- tail_mask: int32 [4096, 5312], P(('groups', 'seq'), 'track'), parts along dimension 0, may hold values 0 or 1
- track_scale: float32 [5312], P('track'), may hold values from 0.5 to 2
Outputs:
- input_grad: bfloat16 [1536, 4096], P('track', ('groups', 'seq')), parts along dimension 1
- taps_grad: float32 [3072, 3], P(('groups', 'track', 'seq')), parts along dimension 0
There are 2 independent parts, one for each index of `groups`. A program takes and returns all parts, laid end to end along the dimension named above; an argument that names none is the same for every part. Nothing has to cross between parts.
Inputs may be any that keep to these rules, and one draw needn't show every extreme that they name: `dilation_level`: every level 0 and 4 occurs.
All inputs are finite; a program needn't handle non-finite values. No bound on the sum of `tail_mask` on one device may be relied on, other than what follows from the above.
Results may differ from a plain program's by a relative error of at most 0.0057.
Values may be sent and summed in bfloat16 or wider, within the bound.
A program may use at most 128 MiB of HBM per device.

v0:
```python
import math

import jax
import jax.numpy as jnp
from jax import lax
from jax.sharding import PartitionSpec as P

DILATION_COUNT = 5
BASE_DILATION = 32


root_half = 0.7071067811865476
norm_const = 0.3989422804014327


def gelu_slope(value):
    return 0.5 * (1.0 + jax.scipy.special.erf(value * root_half)) + value * norm_const * jnp.exp(
        -0.5 * value * value
    )


def taps_at(buffer, onehot, margin, sign):
    width_own = buffer.shape[1] - 2 * margin
    result = jnp.zeros((buffer.shape[0], width_own), jnp.float32)
    for level_index in range(onehot.shape[1]):
        receptive_span = BASE_DILATION * 2**level_index
        begin = margin + sign * receptive_span
        result = (
            result + onehot[:, level_index : level_index + 1] * buffer[:, begin : begin + width_own]
        )
    return result


def spread(values, onehot, margin, sign):
    result = jnp.zeros((values.shape[0], values.shape[1] + 2 * margin), jnp.float32)
    for level_index in range(onehot.shape[1]):
        receptive_span = BASE_DILATION * 2**level_index
        placed = onehot[:, level_index : level_index + 1] * values
        result = result + jnp.pad(
            placed, ((0, 0), (margin + sign * receptive_span, margin - sign * receptive_span))
        )
    return result


def channel_grads(buffer, hidden_grad, taps, onehot, margin):
    width_own = buffer.shape[1] - 2 * margin
    minus_side = taps_at(buffer, onehot, margin, -1)
    center = buffer[:, margin : margin + width_own]
    plus_side = taps_at(buffer, onehot, margin, 1)
    pre_act = taps[:, 0:1] * minus_side + taps[:, 1:2] * center + taps[:, 2:3] * plus_side
    pre_grad = hidden_grad.astype(jnp.float32) * gelu_slope(pre_act)
    taps_part = jnp.stack(
        [
            jnp.sum(pre_grad * minus_side, axis=1),
            jnp.sum(pre_grad * center, axis=1),
            jnp.sum(pre_grad * plus_side, axis=1),
        ],
        axis=1,
    )
    contrib = spread(taps[:, 0:1] * pre_grad, onehot, margin, -1) + spread(
        taps[:, 2:3] * pre_grad, onehot, margin, 1
    )
    contrib = contrib + jnp.pad(taps[:, 1:2] * pre_grad, ((0, 0), (margin, margin)))
    return (contrib, taps_part)


def local(
    section_input,
    conv_taps,
    dilation_level,
    pointwise_matrix,
    head_weight,
    pred_error,
    tail_mask,
    track_scale,
):
    own_channels = section_input.shape[0]
    own_rows = section_input.shape[1]
    adjoint = (
        tail_mask.astype(jnp.float32) * track_scale[None, :] * pred_error.astype(jnp.float32)
    ).astype(jnp.bfloat16)
    full_grad = lax.dot_general(
        lax.all_gather(head_weight, "seq", axis=0, tiled=True),
        adjoint,
        (((1,), (1,)), ((), ())),
        preferred_element_type=jnp.float32,
    )
    total = lax.psum(full_grad, "track")
    out_grad_b = total.astype(jnp.bfloat16)
    out_grad = lax.dynamic_slice_in_dim(
        total, lax.axis_index("track") * own_channels, own_channels, 0
    )
    hidden_grad = jnp.dot(
        lax.all_gather(pointwise_matrix, "seq", axis=1, tiled=True),
        out_grad_b,
        preferred_element_type=jnp.float32,
    ).astype(jnp.bfloat16)
    largest_span = BASE_DILATION * 2 ** (DILATION_COUNT - 1)
    scale = 1.0 / math.sqrt(own_rows * lax.axis_size("seq"))
    onehot = (
        dilation_level[:, None] == jnp.arange(DILATION_COUNT, dtype=jnp.int32)[None, :]
    ).astype(jnp.float32)
    owned_input, owned_grad = (
        lax.all_to_all(section_input, "seq", split_axis=0, concat_axis=1, tiled=True),
        lax.all_to_all(hidden_grad, "seq", split_axis=0, concat_axis=1, tiled=True),
    )
    padded = jnp.pad(owned_input.astype(jnp.float32), ((0, 0), (largest_span, largest_span)))
    contrib, taps_part = channel_grads(padded, owned_grad, conv_taps, onehot, largest_span)
    window = contrib[:, largest_span : largest_span + owned_input.shape[1]]
    conv_part = lax.all_to_all(window, "seq", split_axis=1, concat_axis=0, tiled=True)
    taps_grad = taps_part * scale
    input_grad = (out_grad + conv_part).astype(jnp.bfloat16)
    return (input_grad, taps_grad)


def solution(mesh):
    in_specs = (
        P("track", ("groups", "seq")),
        P(("track", "seq"), None),
        P(("track", "seq")),
        P("track", "seq"),
        P("seq", "track"),
        P(("groups", "seq"), "track"),
        P(("groups", "seq"), "track"),
        P("track"),
    )
    out_specs = (P("track", ("groups", "seq")), P(("groups", "track", "seq"), None))
    return jax.shard_map(local, mesh=mesh, in_specs=in_specs, out_specs=out_specs, check_vma=False)
```

profile of v0, /device:TPU:0, one launch (start us, length us, event | category | flops | bytes accessed | tf_op | source)
XLA Modules:
  0.0 273.3 jit_solution(16173658888297458638)
XLA Ops:
  7.2 0.0 all-gather.3.cloned.1.call-start
  7.2 0.7 all-gather.3.cloned.1.call-update
  7.9 0.0 all-gather.5.cloned.1.call-start
  7.9 0.7 all-gather.5.cloned.1.call-update
  8.6 0.0 all-reduce.14.cloned.1.call-start
  8.7 127.4 %all-gather.3.cloned.1.call-done = bf16[1536,2656]{1,0:T(8,128)(2,1)} async-done(((bf16[192,2656]{1,0:T(8,128)(2,1)}), bf16[1536,2656]{1,0:T(8,128)(2,1)}) %all-gather.3.cloned.1.call-update) | async-done | bytes 8159248 | tf_op jit(solution)/shard_map/all_gather | solution.py:83
  136.1 8.7 %convolution_bitcast_fusion = f32[1536,256]{0,1:T(8,128)} fusion(bf16[1536,2656]{1,0:T(8,128)(2,1)} %all-gather.3.cloned.1.call-done, bf16[256,2656]{0,1:T(8,128)(2,1)} %param.13, s32[256,2656]{0,1:T(8,128)} %param.14, f32[2656]{0:T(1024)} %param.15), kind=kOutput, calls=%fused_computation | convolution fusion | flops 2092163072 | bytes 13822336 | tf_op jit(solution)/shard_map/dot_general | solution.py:82
  144.8 0.0 copy-start.2
  144.8 0.0 copy-start.1
  144.8 0.0 all-reduce.14.cloned.1.call-update
  144.9 3.5 %all-to-all-start.1 = ((bf16[8,96,256]{2,1,0:T(8,128)(2,1)}), bf16[8,96,256]{2,1,0:T(8,128)(2,1)S(1)}, u32[]{:S(2)}, u32[]{:S(2)}) async-start(bf16[8,96,256]{2,1,0:T(8,128)(2,1)} %bitcast.6), calls=%async_computation.1 | async-start | bytes 786432 | tf_op jit(solution)/shard_map/all_to_all | solution.py:104
  148.3 0.0 copy-done.2
  148.4 0.0 copy-done.1
  148.4 46.3 %all-gather.5.cloned.1.call-done = bf16[768,1536]{0,1:T(8,128)(2,1)} async-done(((bf16[768,192]{0,1:T(8,128)(2,1)}), bf16[768,1536]{0,1:T(8,128)(2,1)}) %all-gather.5.cloned.1.call-update) | async-done | bytes 2359312 | tf_op jit(solution)/shard_map/all_gather | solution.py:94
  194.7 21.3 %all-reduce.14.cloned.1.call-done = f32[1536,256]{0,1:T(8,128)} async-done(((f32[1536,256]{0,1:T(8,128)}), f32[1536,256]{0,1:T(8,128)}) %all-reduce.14.cloned.1.call-update) | async-done | bytes 1572880 | tf_op jit(solution)/shard_map/psum | solution.py:88
  216.0 2.9 %fusion.1 = bf16[768,256]{0,1:T(8,128)(2,1)S(1)} fusion(bf16[768,1536]{0,1:T(8,128)(2,1)} %all-gather.5.cloned.1.call-done, f32[1536,256]{0,1:T(8,128)} %all-reduce.14.cloned.1.call-done), kind=kOutput, calls=%fused_computation.14 | convolution fusion | flops 604569600 | bytes 4325376 | tf_op jit(solution)/shard_map/dot_general | solution.py:93
  218.9 0.9 copy.17
  219.9 0.0 all-to-all-done.1
  219.9 5.8 %all-to-all-start = ((bf16[8,96,256]{2,1,0:T(8,128)(2,1)}), bf16[8,96,256]{2,1,0:T(8,128)(2,1)S(1)}, u32[]{:S(2)}, u32[]{:S(2)}) async-start(bf16[8,96,256]{2,1,0:T(8,128)(2,1)} %bitcast.4), calls=%async_computation | async-start | bytes 786432 | tf_op jit(solution)/shard_map/all_to_all | solution.py:105
  225.7 0.1 convert_bitcast_fusion
  225.7 0.1 copy.25
  225.8 1.1 fusion.19
  226.9 10.8 %all-to-all-done = bf16[8,96,256]{2,1,0:T(8,128)(2,1)S(1)} async-done(((bf16[8,96,256]{2,1,0:T(8,128)(2,1)}), bf16[8,96,256]{2,1,0:T(8,128)(2,1)S(1)}, u32[]{:S(2)}, u32[]{:S(2)}) %all-to-all-start) | async-done | bytes 393248 | tf_op jit(solution)/shard_map/all_to_all | solution.py:105
  237.8 0.1 convert_bitcast_fusion.1
  237.9 0.1 copy.24
  237.9 0.8 multiply_reduce_fusion.2
  238.7 1.0 multiply_multiply_fusion.10
  239.7 0.9 pad_add_fusion
  240.6 0.0 copy-start
  240.6 0.9 copy.27
  241.5 3.6 %all-to-all-start.2 = ((f32[96,8,256]{2,0,1:T(8,128)}), f32[96,8,256]{2,0,1:T(8,128)S(1)}, u32[]{:S(2)}, u32[]{:S(2)}) async-start(f32[96,8,256]{2,0,1:T(8,128)} %bitcast.41), calls=%async_computation.2 | async-start | bytes 1572864 | tf_op jit(solution)/shard_map/all_to_all | solution.py:110
  245.1 0.6 maximum_multiply_fusion
  245.7 19.8 %all-to-all-done.2 = f32[96,8,256]{2,0,1:T(8,128)S(1)} async-done(((f32[96,8,256]{2,0,1:T(8,128)}), f32[96,8,256]{2,0,1:T(8,128)S(1)}, u32[]{:S(2)}, u32[]{:S(2)}) %all-to-all-start.2) | async-done | bytes 786464 | tf_op jit(solution)/shard_map/all_to_all | solution.py:110
  265.5 0.3 copy.21
  265.8 0.0 copy-done
  265.8 0.1 add_convert_fusion
  265.9 0.9 copy.22
  (3 shorter events, 0.0 us)
Async XLA Ops:
  7.2 129.0 %all-gather.3.cloned.1.call-start = ((), (), s32[]{:S(2)}) async-start(), calls=%async_computation.3 | async-start | bytes 9289728 | tf_op jit(solution)/shard_map/all_gather | solution.py:83
  7.9 186.8 %all-gather.5.cloned.1.call-start = ((), (), s32[]{:S(2)}) async-start(), calls=%async_computation.5 | async-start | bytes 2654208 | tf_op jit(solution)/shard_map/all_gather | solution.py:94
  8.6 207.4 %all-reduce.14.cloned.1.call-start = ((), (), s32[]{:S(2)}) async-start(), calls=%async_computation.4 | async-start | bytes 3145728 | tf_op jit(solution)/shard_map/psum | solution.py:88
  144.8 3.5 %copy-start.2 = (s32[96]{0:T(128)S(1)}, s32[96]{0:T(128)}, u32[]{:S(2)}) copy-start(s32[96]{0:T(128)} %param.10) | copy-start | bytes 1156
  144.8 3.5 %copy-start.1 = (f32[96,3]{0,1:T(4,128)S(1)}, f32[96,3]{0,1:T(4,128)}, u32[]{:S(2)}) copy-start(f32[96,3]{0,1:T(4,128)} %param.9) | copy-start | bytes 3460
  144.9 75.0 %all-to-all-start.1 = ((bf16[8,96,256]{2,1,0:T(8,128)(2,1)}), bf16[8,96,256]{2,1,0:T(8,128)(2,1)S(1)}, u32[]{:S(2)}, u32[]{:S(2)}) async-start(bf16[8,96,256]{2,1,0:T(8,128)(2,1)} %bitcast.6), calls=%async_computation.1 | async-start | bytes 786432 | tf_op jit(solution)/shard_map/all_to_all | solution.py:104
  219.9 17.9 %all-to-all-start = ((bf16[8,96,256]{2,1,0:T(8,128)(2,1)}), bf16[8,96,256]{2,1,0:T(8,128)(2,1)S(1)}, u32[]{:S(2)}, u32[]{:S(2)}) async-start(bf16[8,96,256]{2,1,0:T(8,128)(2,1)} %bitcast.4), calls=%async_computation | async-start | bytes 786432 | tf_op jit(solution)/shard_map/all_to_all | solution.py:105
  240.6 25.2 %copy-start = (f32[1536,256]{0,1:T(8,128)S(1)}, f32[1536,256]{0,1:T(8,128)}, u32[]{:S(2)}) copy-start(f32[1536,256]{0,1:T(8,128)} %all-reduce.14.cloned.1.call-done) | copy-start | bytes 4718596
  241.5 24.0 %all-to-all-start.2 = ((f32[96,8,256]{2,0,1:T(8,128)}), f32[96,8,256]{2,0,1:T(8,128)S(1)}, u32[]{:S(2)}, u32[]{:S(2)}) async-start(f32[96,8,256]{2,0,1:T(8,128)} %bitcast.41), calls=%async_computation.2 | async-start | bytes 1572864 | tf_op jit(solution)/shard_map/all_to_all | solution.py:110
Sparse Core Ops, SparseCore 0:
  10.2 125.8 all-gather.2
  138.3 56.3 all-gather.4
  197.1 18.9 all-reduce.13
where the time goes:
time: 274 us; the launch traced here: 273 us
  waiting for transfers between devices  227 us (83%)
  between operations  13.9 us (5%)
  starting transfers between devices  13 us (5%)
  matrix products  11.6 us (4%)
  other arithmetic  4.55 us (2%)
  local copies, waits for them, and re-layouts  3.2 us (1%)
    all_gather x1, waiting for transfers between devices, local(): lax.all_gather(head_weight, 'seq', axis=0, tiled=True)  127 us
    all_gather x1, waiting for transfers between devices, local(): lax.all_gather(pointwise_matrix, 'seq', axis=1, tiled=True)  46.3 us
    psum x1, waiting for transfers between devices, local(): total = lax.psum(full_grad, 'track')  21.3 us
    all_to_all x1, waiting for transfers between devices, local(): lax.all_to_all(window, 'seq', split_axis=1, concat_axis=0, tiled=True)  19.8 us
    all_to_all x1, waiting for transfers between devices, local(): lax.all_to_all(hidden_grad, 'seq', split_axis=0, concat_axis=1, tiled=True)  10.8 us
    dot_general x1, matrix products, local(): lax.dot_general(lax.all_gather(head_weight, 'seq', axis=0, tiled=True), a...  8.7 us
    all_to_all x1, starting transfers between devices, local(): lax.all_to_all(hidden_grad, 'seq', split_axis=0, concat_axis=1, tiled=True)  5.78 us
  transfers between devices with their start and end apart: 6, of which 5 were waited for; matrix products, arithmetic and copies ran while one was open for 5% of the time, Pallas kernels for 0%

commit v1 on v0

--- a/solution.py
+++ b/solution.py
@@ -1,8 +1,11 @@
+import functools
 import math
 
 import jax
 import jax.numpy as jnp
 from jax import lax
+from jax.experimental import pallas as pl
+from jax.experimental.pallas import tpu as pltpu
 from jax.sharding import PartitionSpec as P
 
 DILATION_COUNT = 5
@@ -113,6 +116,677 @@
     return (input_grad, taps_grad)
 
 
+MESH = pl.DeviceIdType.MESH
+CROSS = 2
+PARTS = 3
+ADJ_PARTS = 4
+
+
+def fused_kernel(
+    chain,
+    sec,
+    taps,
+    level,
+    pw,
+    hw,
+    err,
+    mask,
+    scale,
+    out,
+    tg,
+    wb,
+    ab,
+    ev,
+    mv,
+    pb,
+    gp,
+    gr,
+    ob,
+    ox,
+    hs,
+    hr,
+    xr,
+    xp,
+    hf,
+    cb,
+    rb,
+    ld_sem,
+    w_send,
+    w_recv,
+    wy_send,
+    wy_recv,
+    p_send,
+    p_recv,
+    py_send,
+    py_recv,
+    a_send,
+    a_recv,
+    g_send,
+    g_recv,
+    o_send,
+    o_recv,
+    x_send,
+    x_recv,
+    h_send,
+    h_recv,
+    r_send,
+    r_recv,
+):
+    g = lax.axis_index("groups")
+    s = lax.axis_index("seq")
+    t = lax.axis_index("track")
+    members = chain * CROSS
+    z = s // CROSS
+    x = s % CROSS
+    head_rows = hw.shape[0]
+    half = head_rows // 2
+    piece = half // PARTS
+    own_rows = err.shape[0]
+    own = sec.shape[0]
+    owned = own // members
+    phalf = own // 2
+    adj_rows = own_rows // ADJ_PARTS
+    pair_rows = CROSS * own_rows
+    length = members * own_rows
+    span = xp.shape[1] - length
+
+    sibling = (g, s, 1 - t)
+    twin = (1 - g, s, t)
+    across = (g, z * CROSS + 1 - x, t)
+
+    def peer(k):
+        return lax.rem(s + k, members)
+
+    barrier = pltpu.get_barrier_semaphore()
+
+    def greet(k, carry):
+        pl.semaphore_signal(barrier, inc=1, device_id=(g, peer(k), t), device_id_type=MESH)
+        return carry
+
+    lax.fori_loop(1, members, greet, 0)
+    pl.semaphore_signal(barrier, inc=1, device_id=sibling, device_id_type=MESH)
+    pl.semaphore_signal(barrier, inc=1, device_id=twin, device_id_type=MESH)
+
+    own_w = pltpu.make_async_copy(
+        hw, wb.at[pl.ds(pl.multiple_of(z * head_rows, 16), head_rows), :], ld_sem.at[0]
+    )
+    own_p = pltpu.make_async_copy(pw, pb.at[z], ld_sem.at[1])
+    own_x = pltpu.make_async_copy(sec.at[pl.ds(pl.multiple_of(s * owned, 16), owned), :], xr.at[s], ld_sem.at[2])
+    loads = []
+    for c in range(ADJ_PARTS):
+        rows = pl.ds(c * adj_rows, adj_rows)
+        loads.append(
+            (
+                pltpu.make_async_copy(err.at[rows, :], ev.at[rows, :], ld_sem.at[3 + 2 * c]),
+                pltpu.make_async_copy(mask.at[rows, :], mv.at[rows, :], ld_sem.at[4 + 2 * c]),
+            )
+        )
+    for first, second in loads:
+        first.start()
+        second.start()
+    own_w.start()
+    own_p.start()
+    own_x.start()
+    pl.semaphore_wait(barrier, members - 1 + 2)
+
+    def w_rows(shard, c, which):
+        return pl.ds(pl.multiple_of(shard * head_rows + which * half + c * piece, 16), piece)
+
+    def w_hop(shard, c, src, toward, direction):
+        slot = shard * PARTS + c
+        return pltpu.make_async_remote_copy(
+            src_ref=src,
+            dst_ref=wb.at[w_rows(shard, c, g), :],
+            send_sem=w_send.at[direction, slot],
+            recv_sem=w_recv.at[slot],
+            device_id=(g, toward * CROSS + x, t),
+            device_id_type=MESH,
+        )
+
+    def w_swap(shard, c, which):
+        slot = shard * PARTS + c
+        block = wb.at[w_rows(shard, c, which), :]
+        return pltpu.make_async_remote_copy(
+            src_ref=block,
+            dst_ref=block,
+            send_sem=wy_send.at[slot],
+            recv_sem=wy_recv.at[slot],
+            device_id=twin,
+            device_id_type=MESH,
+        )
+
+    def p_hop(shard, src, toward, direction):
+        return pltpu.make_async_remote_copy(
+            src_ref=src,
+            dst_ref=pb.at[shard, pl.ds(pl.multiple_of(g * phalf, 16), phalf), :],
+            send_sem=p_send.at[direction, shard],
+            recv_sem=p_recv.at[shard],
+            device_id=(g, toward * CROSS + x, t),
+            device_id_type=MESH,
+        )
+
+    def p_swap(shard, which):
+        block = pb.at[shard, pl.ds(pl.multiple_of(which * phalf, 16), phalf), :]
+        return pltpu.make_async_remote_copy(
+            src_ref=block,
+            dst_ref=block,
+            send_sem=py_send.at[shard],
+            recv_sem=py_recv.at[shard],
+            device_id=twin,
+            device_id_type=MESH,
+        )
+
+    has_up = z < chain - 1
+    has_down = z > 0
+
+    def own_piece(c):
+        return hw.at[pl.ds(pl.multiple_of(g * half + c * piece, 16), piece), :]
+
+    own_phalf = pw.at[pl.ds(pl.multiple_of(g * phalf, 16), phalf), :]
+
+    @pl.when(has_up)
+    def _():
+        for c in range(PARTS):
+            w_hop(z, c, own_piece(c), z + 1, 0).start()
+
+    @pl.when(has_down)
+    def _():
+        for c in range(PARTS):
+            w_hop(z, c, own_piece(c), z - 1, 1).start()
+
+    def a_copy(c):
+        rows = pl.ds(pl.multiple_of(c * adj_rows, 16), adj_rows)
+        block = ab.at[x, rows, :]
+        return pltpu.make_async_remote_copy(
+            src_ref=block,
+            dst_ref=block,
+            send_sem=a_send.at[c],
+            recv_sem=a_recv.at[c],
+            device_id=across,
+            device_id_type=MESH,
+        )
+
+    for c in range(ADJ_PARTS):
+        loads[c][0].wait()
+        loads[c][1].wait()
+
+        def fill(i, carry):
+            rows = pl.ds(pl.multiple_of(c * adj_rows + i * 16, 16), 16)
+            value = mv[rows, :].astype(jnp.float32) * scale[...] * ev[rows, :].astype(jnp.float32)
+            ab[x, rows, :] = value.astype(jnp.bfloat16)
+            return carry
+
+        lax.fori_loop(0, adj_rows // 16, fill, 0)
+        a_copy(c).start()
+
+    @pl.when(has_up)
+    def _():
+        p_hop(z, own_phalf, z + 1, 0).start()
+
+    @pl.when(has_down)
+    def _():
+        p_hop(z, own_phalf, z - 1, 1).start()
+
+    def x_copy(to, frm):
+        return pltpu.make_async_remote_copy(
+            src_ref=sec.at[pl.ds(pl.multiple_of(to * owned, 16), owned), :],
+            dst_ref=xr.at[frm],
+            send_sem=x_send.at[to],
+            recv_sem=x_recv.at[frm],
+            device_id=(g, to, t),
+            device_id_type=MESH,
+        )
+
+    def x_start(k, carry):
+        x_copy(peer(k), s).start()
+        return carry
+
+    lax.fori_loop(1, members, x_start, 0)
+
+    below = z
+    above = chain - 1 - z
+    near = jnp.minimum(below, above)
+
+    def order(j):
+        step = (j + 1) // 2
+        alternate = jnp.where(j % 2 == 1, z - step, z + step)
+        one_sided = jnp.where(above > below, z + (j - near), z - (j - near))
+        return jnp.where(j <= 2 * near, alternate, one_sided)
+
+    def g_copy(shard, xs):
+        rows = pl.ds(pl.multiple_of(shard * head_rows, 16), head_rows)
+        return pltpu.make_async_remote_copy(
+            src_ref=gp.at[xs, rows, :],
+            dst_ref=gr.at[xs, rows, :],
+            send_sem=g_send.at[shard, xs],
+            recv_sem=g_recv.at[shard, xs],
+            device_id=sibling,
+            device_id_type=MESH,
+        )
+
+    def head_dot(shard, xs):
+        rows = pl.ds(pl.multiple_of(shard * head_rows, 16), head_rows)
+        gp[xs, rows, :] = lax.dot_general(
+            wb[rows, :],
+            ab[xs],
+            (((1,), (1,)), ((), ())),
+            preferred_element_type=jnp.float32,
+        )
+        g_copy(shard, xs).start()
+
+    def w_relay(e, carry):
+        paired = (near >= 1) & (e < 2 * PARTS)
+        j = jnp.where(paired, 1 + e % 2, e // PARTS + 1)
+        c = jnp.where(paired, e // 2, e % PARTS)
+        shard = order(j)
+        block = wb.at[w_rows(shard, c, g), :]
+        w_hop(shard, c, block, z, 0).wait_recv()
+
+        @pl.when((shard < z) & has_up)
+        def _():
+            w_hop(shard, c, block, z + 1, 0).start()
+
+        @pl.when((shard > z) & has_down)
+        def _():
+            w_hop(shard, c, block, z - 1, 1).start()
+
+        w_swap(shard, c, g).start()
+        return carry
+
+    def wait_swaps(shard):
+        def one(c, carry):
+            w_swap(shard, c, 1 - g).wait_recv()
+            return carry
+
+        lax.fori_loop(0, PARTS, one, 0)
+
+    own_w.wait()
+    head_dot(z, x)
+    steps = chain - 1
+    lax.fori_loop(0, (steps - 1) * PARTS, w_relay, 0)
+
+    def early(j, carry):
+        shard = order(j)
+        wait_swaps(shard)
+        head_dot(shard, x)
+        return carry
+
+    lax.fori_loop(1, steps - 1, early, 0)
+    lax.fori_loop((steps - 1) * PARTS, steps * PARTS, w_relay, 0)
+    lax.fori_loop(jnp.maximum(steps - 1, 1), steps, early, 0)
+
+    def a_wait(c, carry):
+        rows = pl.ds(pl.multiple_of(c * adj_rows, 16), adj_rows)
+        block = ab.at[1 - x, rows, :]
+        pltpu.make_async_remote_copy(
+            src_ref=block,
+            dst_ref=block,
+            send_sem=a_send.at[c],
+            recv_sem=a_recv.at[c],
+            device_id=across,
+            device_id_type=MESH,
+        ).wait_recv()
+        return carry
+
+    lax.fori_loop(0, ADJ_PARTS, a_wait, 0)
+
+    def late(j, carry):
+        head_dot(jnp.where(j == 0, z, order(jnp.maximum(j, 1))), 1 - x)
+        return carry
+
+    lax.fori_loop(0, steps, late, 0)
+
+    def p_relay(j, carry):
+        shard = order(j)
+        block = pb.at[shard, pl.ds(pl.multiple_of(g * phalf, 16), phalf), :]
+        p_hop(shard, block, z, 0).wait_recv()
+
+        @pl.when((shard < z) & has_up)
+        def _():
+            p_hop(shard, block, z + 1, 0).start()
+
+        @pl.when((shard > z) & has_down)
+        def _():
+            p_hop(shard, block, z - 1, 1).start()
+
+        p_swap(shard, g).start()
+        return carry
+
+    lax.fori_loop(1, steps + 1, p_relay, 0)
+    last = order(steps)
+    wait_swaps(last)
+    head_dot(last, x)
+    head_dot(last, 1 - x)
+
+    def core_sum(j, carry):
+        shard = jnp.where(j == 0, z, order(jnp.maximum(j, 1)))
+        rows = pl.ds(pl.multiple_of(shard * head_rows, 16), head_rows)
+        for xs in range(CROSS):
+            g_copy(shard, xs).wait_recv()
+            ob[rows, xs * own_rows : (xs + 1) * own_rows] = (gp[xs, rows, :] + gr[xs, rows, :]).astype(
+                jnp.bfloat16
+            )
+        return carry
+
+    lax.fori_loop(0, chain, core_sum, 0)
+
+    blocks_kept = chain // 2
+
+    def o_copy(q):
+        return pltpu.make_async_remote_copy(
+            src_ref=ob.at[
+                pl.ds(pl.multiple_of((t * blocks_kept + q) * head_rows, 16), head_rows),
+                pl.ds(pl.multiple_of((1 - x) * own_rows, 128), own_rows),
+            ],
+            dst_ref=ox.at[q],
+            send_sem=o_send.at[q],
+            recv_sem=o_recv.at[q],
+            device_id=across,
+            device_id_type=MESH,
+        )
+
+    for q in range(blocks_kept):
+        o_copy(q).start()
+
+    own_p.wait()
+
+    def p_wait(j, carry):
+        p_swap(order(j), 1 - g).wait_recv()
+        return carry
+
+    lax.fori_loop(1, steps + 1, p_wait, 0)
+
+    def hidden_for(to):
+        rows = pl.ds(pl.multiple_of(to * owned, 16), owned)
+        total = jnp.zeros((owned, pair_rows), jnp.float32)
+        for shard in range(chain):
+            total = total + jnp.dot(
+                pb[shard, rows, :],
+                ob[shard * head_rows : (shard + 1) * head_rows, :],
+                preferred_element_type=jnp.float32,
+            )
+        return total.astype(jnp.bfloat16)
+
+    def h_copy(to, frm):
+        return pltpu.make_async_remote_copy(
+            src_ref=hs.at[to],
+            dst_ref=hr.at[frm],
+            send_sem=h_send.at[to],
+            recv_sem=h_recv.at[frm],
+            device_id=(g, to, t),
+            device_id_type=MESH,
+        )
+
+    def h_step(k, carry):
+        to = peer(k)
+        hs[to] = hidden_for(to)
+        h_copy(to, s).start()
+        return carry
+
+    lax.fori_loop(1, members, h_step, 0)
+    hr[s] = hidden_for(s)
+
+    own_x.wait()
+
+    def x_wait(k, carry):
+        x_copy(s, peer(k)).wait_recv()
+        return carry
+
+    lax.fori_loop(1, members, x_wait, 0)
+    for m in range(members):
+        xp[:, m * own_rows : (m + 1) * own_rows] = xr[m].astype(jnp.float32)
+    xp[:, length:] = jnp.zeros((owned, span), jnp.float32)
+
+    def h_wait(k, carry):
+        h_copy(s, peer(k)).wait_recv()
+        return carry
+
+    lax.fori_loop(1, members, h_wait, 0)
+    for m in range(chain):
+        both = hr[CROSS * m].astype(jnp.float32) + hr[CROSS * m + 1].astype(jnp.float32)
+        hf[:, m * pair_rows : (m + 1) * pair_rows] = both.astype(jnp.bfloat16)
+
+    padded = length + span
+    norm = 1.0 / math.sqrt(length)
+
+    def conv_rows(i, carry):
+        rows = pl.ds(pl.multiple_of(i * 16, 16), 16)
+        lev = level[rows, :]
+        tap = taps[rows, :]
+
+        def pick(value, sign):
+            result = None
+            for k in range(DILATION_COUNT):
+                reach = BASE_DILATION * 2**k
+                moved = pltpu.roll(value, reach if sign < 0 else padded - reach, 1)[:, :length]
+                result = moved if result is None else jnp.where(lev == k, moved, result)
+            return result
+
+        wide = xp[rows, :]
+        minus = pick(wide, -1)
+        plus = pick(wide, 1)
+        center = wide[:, :length]
+        pre_act = tap[:, 0:1] * minus + tap[:, 1:2] * center + tap[:, 2:3] * plus
+        pre_grad = hf[rows, :].astype(jnp.float32) * gelu_slope(pre_act)
+        tg[rows, 0:1] = jnp.sum(pre_grad * minus, axis=1, keepdims=True) * norm
+        tg[rows, 1:2] = jnp.sum(pre_grad * center, axis=1, keepdims=True) * norm
+        tg[rows, 2:3] = jnp.sum(pre_grad * plus, axis=1, keepdims=True) * norm
+        spread_wide = jnp.concatenate([pre_grad, jnp.zeros((16, span), jnp.float32)], axis=1)
+        part = (
+            tap[:, 0:1] * pick(spread_wide, 1)
+            + tap[:, 1:2] * pre_grad
+            + tap[:, 2:3] * pick(spread_wide, -1)
+        ).astype(jnp.bfloat16)
+        for m in range(members):
+            cb[m, rows, :] = part[:, m * own_rows : (m + 1) * own_rows]
+        return carry
+
+    lax.fori_loop(0, owned // 16, conv_rows, 0)
+
+    def r_copy(to, frm):
+        return pltpu.make_async_remote_copy(
+            src_ref=cb.at[to],
+            dst_ref=rb.at[frm],
+            send_sem=r_send.at[to],
+            recv_sem=r_recv.at[frm],
+            device_id=(g, to, t),
+            device_id_type=MESH,
+        )
+
+    def r_start(k, carry):
+        r_copy(peer(k), s).start()
+        return carry
+
+    lax.fori_loop(1, members, r_start, 0)
+    rb[s] = cb[s]
+    for q in range(blocks_kept):
+        o_copy(q).wait_recv()
+
+    def r_wait(k, carry):
+        r_copy(s, peer(k)).wait_recv()
+        return carry
+
+    lax.fori_loop(1, members, r_wait, 0)
+
+    per = head_rows // owned
+    for q in range(blocks_kept):
+        for u in range(per):
+            mine = (CROSS * q + x) * per + u
+            src = pl.ds(pl.multiple_of((t * blocks_kept + q) * head_rows + u * owned, 16), owned)
+            here = jnp.where(
+                x == 0, ob[src, 0:own_rows].astype(jnp.float32), ob[src, own_rows:].astype(jnp.float32)
+            )
+            out[pl.ds(pl.multiple_of(mine * owned, 16), owned), :] = (
+                here + rb[mine].astype(jnp.float32)
+            ).astype(jnp.bfloat16)
+            other = (CROSS * q + 1 - x) * per + u
+            there = ox[q, u * owned : (u + 1) * owned, :].astype(jnp.float32)
+            out[pl.ds(pl.multiple_of(other * owned, 16), owned), :] = (
+                there + rb[other].astype(jnp.float32)
+            ).astype(jnp.bfloat16)
+
+    def w_done(shard, carry):
+        def one(c, inner):
+            block = wb.at[w_rows(shard, c, g), :]
+
+            @pl.when((shard <= z) & has_up)
+            def _():
+                w_hop(shard, c, block, z, 0).wait_send()
+
+            @pl.when((shard >= z) & has_down)
+            def _():
+                w_hop(shard, c, block, z, 1).wait_send()
+
+            @pl.when(shard != z)
+            def _():
+                w_swap(shard, c, g).wait_send()
+
+            return inner
+
+        lax.fori_loop(0, PARTS, one, 0)
+        pblock = pb.at[shard, pl.ds(pl.multiple_of(g * phalf, 16), phalf), :]
+
+        @pl.when((shard <= z) & has_up)
+        def _():
+            p_hop(shard, pblock, z, 0).wait_send()
+
+        @pl.when((shard >= z) & has_down)
+        def _():
+            p_hop(shard, pblock, z, 1).wait_send()
+
+        @pl.when(shard != z)
+        def _():
+            p_swap(shard, g).wait_send()
+
+        for xs in range(CROSS):
+            g_copy(shard, xs).wait_send()
+        return carry
+
+    lax.fori_loop(0, chain, w_done, 0)
+
+    def a_done(c, carry):
+        a_copy(c).wait_send()
+        return carry
+
+    lax.fori_loop(0, ADJ_PARTS, a_done, 0)
+    for q in range(blocks_kept):
+        o_copy(q).wait_send()
+
+    def done(k, carry):
+        x_copy(peer(k), s).wait_send()
+        h_copy(peer(k), s).wait_send()
+        r_copy(peer(k), s).wait_send()
+        return carry
+
+    lax.fori_loop(1, members, done, 0)
+
+
+def fused(
+    chain,
+    section_input,
+    conv_taps,
+    dilation_level,
+    pointwise_matrix,
+    head_weight,
+    pred_error,
+    tail_mask,
+    track_scale,
+):
+    own, own_rows = section_input.shape
+    members = chain * CROSS
+    owned = own // members
+    head_rows, tracks = head_weight.shape
+    pair_rows = CROSS * own_rows
+    length = members * own_rows
+    span = BASE_DILATION * 2 ** (DILATION_COUNT - 1)
+    cols = pointwise_matrix.shape[1]
+    bf16, f32 = jnp.bfloat16, jnp.float32
+    dma = pltpu.SemaphoreType.DMA
+    anywhere = pl.BlockSpec(memory_space=pl.ANY)
+    vmem = pl.BlockSpec(memory_space=pltpu.VMEM)
+    return tuple(
+        pl.pallas_call(
+            functools.partial(fused_kernel, chain),
+            out_shape=(
+                jax.ShapeDtypeStruct((own, own_rows), bf16),
+                jax.ShapeDtypeStruct((owned, 3), f32),
+            ),
+            in_specs=[anywhere, vmem, vmem, anywhere, anywhere, anywhere, anywhere, vmem],
+            out_specs=(vmem, vmem),
+            scratch_shapes=[
+                pltpu.VMEM((chain * head_rows, tracks), bf16),
+                pltpu.VMEM((CROSS, own_rows, tracks), bf16),
+                pltpu.VMEM((own_rows, tracks), bf16),
+                pltpu.VMEM((own_rows, tracks), jnp.int32),
+                pltpu.VMEM((chain, own, cols), bf16),
+                pltpu.VMEM((CROSS, chain * head_rows, own_rows), f32),
+                pltpu.VMEM((CROSS, chain * head_rows, own_rows), f32),
+                pltpu.VMEM((chain * head_rows, pair_rows), bf16),
+                pltpu.VMEM((chain // 2, head_rows, own_rows), bf16),
+                pltpu.VMEM((members, owned, pair_rows), bf16),
+                pltpu.VMEM((members, owned, pair_rows), bf16),
+                pltpu.VMEM((members, owned, own_rows), bf16),
+                pltpu.VMEM((owned, length + span), f32),
+                pltpu.VMEM((owned, length), bf16),
+                pltpu.VMEM((members, owned, own_rows), bf16),
+                pltpu.VMEM((members, owned, own_rows), bf16),
+                dma((3 + 2 * ADJ_PARTS,)),
+                dma((2, chain * PARTS)),
+                dma((chain * PARTS,)),
+                dma((chain * PARTS,)),
+                dma((chain * PARTS,)),
+                dma((2, chain)),
+                dma((chain,)),
+                dma((chain,)),
+                dma((chain,)),
+                dma((ADJ_PARTS,)),
+                dma((ADJ_PARTS,)),
+                dma((chain, CROSS)),
+                dma((chain, CROSS)),
+                dma((chain // 2,)),
+                dma((chain // 2,)),
+                dma((members,)),
+                dma((members,)),
+                dma((members,)),
+                dma((members,)),
+                dma((members,)),
+                dma((members,)),
+            ],
+            compiler_params=pltpu.CompilerParams(
+                collective_id=0, has_side_effects=True, vmem_limit_bytes=48 * 1024 * 1024
+            ),
+            name="fused_section",
+        )(
+            section_input,
+            conv_taps,
+            dilation_level[:, None],
+            pointwise_matrix,
+            head_weight,
+            pred_error,
+            tail_mask,
+            track_scale[None, :],
+        )
+    )
+
+
+def local_or_fused(sizes, *args):
+    section_input, head_weight, pred_error = args[0], args[4], args[5]
+    seq = sizes["seq"]
+    fits = (
+        sizes["groups"] == 2
+        and sizes["track"] == 2
+        and seq == 8
+        and head_weight.shape[0] % (2 * PARTS * 16) == 0
+        and section_input.shape[0] % (seq * 16) == 0
+        and section_input.shape[1] % 128 == 0
+        and pred_error.shape[0] % (ADJ_PARTS * 16) == 0
+        and head_weight.shape[0] % (section_input.shape[0] // seq) == 0
+    )
+    if fits:
+        return fused(seq // CROSS, *args)
+    return local(*args)
+
+
 def solution(mesh):
     in_specs = (
         P("track", ("groups", "seq")),
@@ -124,5 +798,7 @@
         P(("groups", "seq"), "track"),
         P("track"),
     )
+    sizes = dict(mesh.shape)
+    body = functools.partial(local_or_fused, sizes)
     out_specs = (P("track", ("groups", "seq")), P(("groups", "track", "seq"), None))
-    return jax.shard_map(local, mesh=mesh, in_specs=in_specs, out_specs=out_specs, check_vma=False)
+    return jax.shard_map(body, mesh=mesh, in_specs=in_specs, out_specs=out_specs, check_vma=False)

time: 274 us -> 109 us (0.40)
  waiting for transfers between devices: 227 us -> 0 us
  Pallas kernels: 0 us -> 95.9 us
  between operations: 13.9 us -> 0.68 us
  starting transfers between devices: 13 us -> 0 us
  matrix products: 11.6 us -> 0 us
  local copies, waits for them, and re-layouts: 3.2 us -> 11.8 us
  other arithmetic: 4.55 us -> 0 us
    all_gather x2 -> x0, waiting for transfers between devices: 174 us -> none  [the longest x1 127 us: local(): lax.all_gather(head_weight, 'seq', axis=0, tiled=True)]
    pallas_call x0 -> x1, Pallas kernels: none -> 95.9 us  [fused(): pl.pallas_call(functools.partial(fused_kernel, chain), out_shape=(jax.Sha...]
    all_to_all x3 -> x0, waiting for transfers between devices: 30.6 us -> none  [the longest x1 19.8 us: local(): lax.all_to_all(window, 'seq', split_axis=1, concat_axis=0, tiled=True)]
    psum x1 -> x0, waiting for transfers between devices: 21.3 us -> none  [local(): total = lax.psum(full_grad, 'track')]
    all_to_all x3 -> x0, starting transfers between devices: 12.9 us -> none  [the longest x1 5.78 us: local(): lax.all_to_all(hidden_grad, 'seq', split_axis=0, concat_axis=1, tiled=True)]
    dot_general x2 -> x0, matrix products: 11.6 us -> none  [the longest x1 8.7 us: local(): lax.dot_general(lax.all_gather(head_weight, 'seq', axis=0, tiled=True), a...]
    unnamed x7 -> x11, local copies, waits for them, and re-layouts: 0.93 us -> 9.67 us
  transfers between devices with their start and end apart: 6 -> 0, of which waited for: 5 -> 0; matrix products, arithmetic and copies ran while one was open for 5% -> 0% of each run, Pallas kernels for 0% -> 0%
where the time goes in v1:
time: 109 us; the launch traced here: 108 us
  Pallas kernels  95.9 us (88%)
  local copies, waits for them, and re-layouts  11.8 us (11%)
    pallas_call x1, Pallas kernels, fused(): pl.pallas_call(functools.partial(fused_kernel, chain), out_shape=(jax.Sha...  95.9 us
    unnamed x11, local copies, waits for them, and re-layouts  9.67 us

profile of v1, /device:TPU:0, one launch (start us, length us, event | category | flops | bytes accessed | tf_op | source)
XLA Modules:
  0.0 108.4 jit_solution(17541741252254452222)
XLA Ops:
  0.6 0.7 broadcast_in_dim.7.scale
  1.3 0.8 copy.10.taps
  2.1 0.8 copy.11.level
  2.9 1.1 %copy.12.pw = bf16[768,192]{1,0:T(8,128)(2,1)S(1)} copy(bf16[768,192]{0,1:T(8,128)(2,1)} %param.11) | data formatting | bytes 589824 | tf_op args[3]
  4.0 1.8 %copy.13.err = bf16[256,2656]{1,0:T(8,128)(2,1)S(1)} copy(bf16[256,2656]{0,1:T(8,128)(2,1)} %param.13) | data formatting | bytes 2719744 | tf_op args[5]
  5.8 0.0 copy-start
  5.8 0.0 copy-start.1
  5.8 3.4 %copy.14.mask = s32[256,2656]{1,0:T(8,128)} copy(s32[256,2656]{0,1:T(8,128)} %param.14) | data formatting | bytes 5439488 | tf_op args[6]
  9.3 0.0 copy-done
  9.3 0.0 copy-done.1
  9.3 95.9 %fused_section.1 = (bf16[768,256]{1,0:T(8,128)(2,1)S(1)}, f32[96,3]{1,0:T(8,128)S(1)}) custom-call(bf16[768,256]{1,0:T(8,128)(2,1)S(1)} %copy-done.1, f32[96,3]{1,0:T(8,128)S(1)} %copy.10.taps, s32[96,1]{1,0:T(8,128)S(1)} %copy.11.level, bf16[768,192]{1,0:T(8,128)(2,1)S(1)} %copy.12.pw, bf16[192,2656]{1,0:T(8,128)(2,1)S(1)} %copy-done, ...), custom_call_target="tpu_custom_call" | custom-call | tf_op jit(solution)/shard_map/fused_section/pallas_call | solution.py:708
  105.2 0.0 copy-start.2
  105.2 0.7 copy-done.2
  105.9 0.7 copy.15
  106.6 1.8 %copy.17 = bf16[768,256]{1,0:T(8,128)(2,1)} copy(bf16[768,256]{1,0:T(8,128)(2,1)} %copy-done.2) | data formatting | bytes 786432
Async XLA Ops:
  5.8 3.5 %copy-start = (bf16[192,2656]{1,0:T(8,128)(2,1)S(1)}, bf16[192,2656]{1,0:T(8,128)(2,1)}, u32[]{:S(2)}) copy-start(bf16[192,2656]{1,0:T(8,128)(2,1)} %hw.1) | copy-start | bytes 3059716
  5.8 3.5 %copy-start.1 = (bf16[768,256]{1,0:T(8,128)(2,1)S(1)}, bf16[768,256]{1,0:T(8,128)(2,1)}, u32[]{:S(2)}) copy-start(bf16[768,256]{1,0:T(8,128)(2,1)} %sec.1) | copy-start | bytes 1179652
  105.2 0.8 copy-start.2

commit v2 on v1

--- a/solution.py
+++ b/solution.py
@@ -150,6 +150,8 @@
     hf,
     cb,
     rb,
+    cols,
+    sums,
     ld_sem,
     w_send,
     w_recv,
@@ -181,11 +183,12 @@
     head_rows = hw.shape[0]
     half = head_rows // 2
     piece = half // PARTS
-    own_rows = err.shape[0]
+    tracks, own_rows = err.shape
     own = sec.shape[0]
     owned = own // members
-    phalf = own // 2
-    adj_rows = own_rows // ADJ_PARTS
+    phalf = pw.shape[0] // 2
+    step = tracks // ADJ_PARTS // 128 * 128
+    cuts = [c * step for c in range(ADJ_PARTS)] + [tracks]
     pair_rows = CROSS * own_rows
     length = members * own_rows
     span = xp.shape[1] - length
@@ -214,7 +217,7 @@
     own_x = pltpu.make_async_copy(sec.at[pl.ds(pl.multiple_of(s * owned, 16), owned), :], xr.at[s], ld_sem.at[2])
     loads = []
     for c in range(ADJ_PARTS):
-        rows = pl.ds(c * adj_rows, adj_rows)
+        rows = pl.ds(cuts[c], cuts[c + 1] - cuts[c])
         loads.append(
             (
                 pltpu.make_async_copy(err.at[rows, :], ev.at[rows, :], ld_sem.at[3 + 2 * c]),
@@ -295,7 +298,7 @@
             w_hop(z, c, own_piece(c), z - 1, 1).start()
 
     def a_copy(c):
-        rows = pl.ds(pl.multiple_of(c * adj_rows, 16), adj_rows)
+        rows = pl.ds(cuts[c], cuts[c + 1] - cuts[c])
         block = ab.at[x, rows, :]
         return pltpu.make_async_remote_copy(
             src_ref=block,
@@ -310,13 +313,24 @@
         loads[c][0].wait()
         loads[c][1].wait()
 
-        def fill(i, carry):
-            rows = pl.ds(pl.multiple_of(c * adj_rows + i * 16, 16), 16)
-            value = mv[rows, :].astype(jnp.float32) * scale[...] * ev[rows, :].astype(jnp.float32)
+        def fill(begin, count):
+            rows = pl.ds(begin, count)
+            line = scale[:, rows]
+            if count < 128:
+                line = jnp.concatenate([line, jnp.zeros((1, 128 - count), jnp.float32)], axis=1)
+            column = jnp.transpose(jnp.broadcast_to(line, (128, 128)))[:count]
+            column = jnp.concatenate([column] * (own_rows // 128), axis=1)
+            value = mv[rows, :].astype(jnp.float32) * column * ev[rows, :].astype(jnp.float32)
             ab[x, rows, :] = value.astype(jnp.bfloat16)
+
+        def fill_step(i, carry):
+            fill(pl.multiple_of(cuts[c] + i * 128, 128), 128)
             return carry
 
-        lax.fori_loop(0, adj_rows // 16, fill, 0)
+        whole, rest = divmod(cuts[c + 1] - cuts[c], 128)
+        lax.fori_loop(0, whole, fill_step, 0)
+        if rest:
+            fill(cuts[c] + whole * 128, rest)
         a_copy(c).start()
 
     @pl.when(has_up)
@@ -369,7 +383,7 @@
         gp[xs, rows, :] = lax.dot_general(
             wb[rows, :],
             ab[xs],
-            (((1,), (1,)), ((), ())),
+            (((1,), (0,)), ((), ())),
             preferred_element_type=jnp.float32,
         )
         g_copy(shard, xs).start()
@@ -415,9 +429,8 @@
     lax.fori_loop((steps - 1) * PARTS, steps * PARTS, w_relay, 0)
     lax.fori_loop(jnp.maximum(steps - 1, 1), steps, early, 0)
 
-    def a_wait(c, carry):
-        rows = pl.ds(pl.multiple_of(c * adj_rows, 16), adj_rows)
-        block = ab.at[1 - x, rows, :]
+    for c in range(ADJ_PARTS):
+        block = ab.at[1 - x, pl.ds(cuts[c], cuts[c + 1] - cuts[c]), :]
         pltpu.make_async_remote_copy(
             src_ref=block,
             dst_ref=block,
@@ -426,9 +439,6 @@
             device_id=across,
             device_id_type=MESH,
         ).wait_recv()
-        return carry
-
-    lax.fori_loop(0, ADJ_PARTS, a_wait, 0)
 
     def late(j, carry):
         head_dot(jnp.where(j == 0, z, order(jnp.maximum(j, 1))), 1 - x)
@@ -496,20 +506,12 @@
 
     lax.fori_loop(1, steps + 1, p_wait, 0)
 
-    def hidden_for(to):
-        rows = pl.ds(pl.multiple_of(to * owned, 16), owned)
-        total = jnp.zeros((owned, pair_rows), jnp.float32)
-        for shard in range(chain):
-            total = total + jnp.dot(
-                pb[shard, rows, :],
-                ob[shard * head_rows : (shard + 1) * head_rows, :],
-                preferred_element_type=jnp.float32,
-            )
-        return total.astype(jnp.bfloat16)
+    def h_rows(to):
+        return pl.ds(pl.multiple_of(to * owned, 16), owned)
 
     def h_copy(to, frm):
         return pltpu.make_async_remote_copy(
-            src_ref=hs.at[to],
+            src_ref=hs.at[h_rows(to), :],
             dst_ref=hr.at[frm],
             send_sem=h_send.at[to],
             recv_sem=h_recv.at[frm],
@@ -517,14 +519,32 @@
             device_id_type=MESH,
         )
 
+    group = members // 2
+    wide_rows = group * owned
+
     def h_step(k, carry):
-        to = peer(k)
-        hs[to] = hidden_for(to)
-        h_copy(to, s).start()
-        return carry
-
-    lax.fori_loop(1, members, h_step, 0)
-    hr[s] = hidden_for(s)
+        n = (s // group + 1 + k) % 2
+        lanes = pl.ds(pl.multiple_of(n * wide_rows, 128), wide_rows)
+        total = jnp.zeros((wide_rows, pair_rows), jnp.float32)
+        for shard in range(chain):
+            total = total + lax.dot_general(
+                pb[shard, :, lanes],
+                ob[shard * head_rows : (shard + 1) * head_rows, :],
+                (((0,), (0,)), ((), ())),
+                preferred_element_type=jnp.float32,
+            )
+        hs[lanes, :] = total.astype(jnp.bfloat16)
+        for u in range(group):
+            to = n * group + u
+
+            @pl.when(to != s)
+            def _():
+                h_copy(to, s).start()
+
+        return carry
+
+    lax.fori_loop(0, 2, h_step, 0)
+    hr[s] = hs[h_rows(s), :]
 
     own_x.wait()
 
@@ -546,20 +566,27 @@
         both = hr[CROSS * m].astype(jnp.float32) + hr[CROSS * m + 1].astype(jnp.float32)
         hf[:, m * pair_rows : (m + 1) * pair_rows] = both.astype(jnp.bfloat16)
 
+    columns = cols.at[1]
+    cols[0] = jnp.zeros((128, 128), jnp.float32)
+    cols[0, 0:3, 0:owned] = taps[...]
+    cols[0, 3:4, 0:owned] = level[...].astype(jnp.float32)
+    cols[1] = jnp.transpose(cols[0])
+    sums[...] = jnp.zeros((128, 128), jnp.float32)
+
     padded = length + span
     norm = 1.0 / math.sqrt(length)
 
     def conv_rows(i, carry):
         rows = pl.ds(pl.multiple_of(i * 16, 16), 16)
-        lev = level[rows, :]
-        tap = taps[rows, :]
+        lev = columns[rows, 3:4]
+        tap = columns[rows, 0:3]
 
         def pick(value, sign):
             result = None
             for k in range(DILATION_COUNT):
                 reach = BASE_DILATION * 2**k
                 moved = pltpu.roll(value, reach if sign < 0 else padded - reach, 1)[:, :length]
-                result = moved if result is None else jnp.where(lev == k, moved, result)
+                result = moved if result is None else jnp.where(lev == float(k), moved, result)
             return result
 
         wide = xp[rows, :]
@@ -568,9 +595,9 @@
         center = wide[:, :length]
         pre_act = tap[:, 0:1] * minus + tap[:, 1:2] * center + tap[:, 2:3] * plus
         pre_grad = hf[rows, :].astype(jnp.float32) * gelu_slope(pre_act)
-        tg[rows, 0:1] = jnp.sum(pre_grad * minus, axis=1, keepdims=True) * norm
-        tg[rows, 1:2] = jnp.sum(pre_grad * center, axis=1, keepdims=True) * norm
-        tg[rows, 2:3] = jnp.sum(pre_grad * plus, axis=1, keepdims=True) * norm
+        sums[rows, 0:1] = jnp.sum(pre_grad * minus, axis=1, keepdims=True) * norm
+        sums[rows, 1:2] = jnp.sum(pre_grad * center, axis=1, keepdims=True) * norm
+        sums[rows, 2:3] = jnp.sum(pre_grad * plus, axis=1, keepdims=True) * norm
         spread_wide = jnp.concatenate([pre_grad, jnp.zeros((16, span), jnp.float32)], axis=1)
         part = (
             tap[:, 0:1] * pick(spread_wide, 1)
@@ -625,6 +652,8 @@
                 there + rb[other].astype(jnp.float32)
             ).astype(jnp.bfloat16)
 
+    tg[...] = jnp.transpose(sums[...])[0:3, 0:owned]
+
     def w_done(shard, carry):
         def one(c, inner):
             block = wb.at[w_rows(shard, c, g), :]
@@ -664,11 +693,8 @@
 
     lax.fori_loop(0, chain, w_done, 0)
 
-    def a_done(c, carry):
+    for c in range(ADJ_PARTS):
         a_copy(c).wait_send()
-        return carry
-
-    lax.fori_loop(0, ADJ_PARTS, a_done, 0)
     for q in range(blocks_kept):
         o_copy(q).wait_send()
 
@@ -702,34 +728,36 @@
     cols = pointwise_matrix.shape[1]
     bf16, f32 = jnp.bfloat16, jnp.float32
     dma = pltpu.SemaphoreType.DMA
-    anywhere = pl.BlockSpec(memory_space=pl.ANY)
+    anywhere = pl.BlockSpec(memory_space=pltpu.HBM)
     vmem = pl.BlockSpec(memory_space=pltpu.VMEM)
-    return tuple(
+    input_grad, taps_grad = (
         pl.pallas_call(
             functools.partial(fused_kernel, chain),
             out_shape=(
                 jax.ShapeDtypeStruct((own, own_rows), bf16),
-                jax.ShapeDtypeStruct((owned, 3), f32),
+                jax.ShapeDtypeStruct((3, owned), f32),
             ),
             in_specs=[anywhere, vmem, vmem, anywhere, anywhere, anywhere, anywhere, vmem],
             out_specs=(vmem, vmem),
             scratch_shapes=[
                 pltpu.VMEM((chain * head_rows, tracks), bf16),
-                pltpu.VMEM((CROSS, own_rows, tracks), bf16),
-                pltpu.VMEM((own_rows, tracks), bf16),
-                pltpu.VMEM((own_rows, tracks), jnp.int32),
-                pltpu.VMEM((chain, own, cols), bf16),
+                pltpu.VMEM((CROSS, tracks, own_rows), bf16),
+                pltpu.VMEM((tracks, own_rows), bf16),
+                pltpu.VMEM((tracks, own_rows), jnp.int32),
+                pltpu.VMEM((chain, cols, own), bf16),
                 pltpu.VMEM((CROSS, chain * head_rows, own_rows), f32),
                 pltpu.VMEM((CROSS, chain * head_rows, own_rows), f32),
                 pltpu.VMEM((chain * head_rows, pair_rows), bf16),
                 pltpu.VMEM((chain // 2, head_rows, own_rows), bf16),
-                pltpu.VMEM((members, owned, pair_rows), bf16),
+                pltpu.VMEM((own, pair_rows), bf16),
                 pltpu.VMEM((members, owned, pair_rows), bf16),
                 pltpu.VMEM((members, owned, own_rows), bf16),
                 pltpu.VMEM((owned, length + span), f32),
                 pltpu.VMEM((owned, length), bf16),
                 pltpu.VMEM((members, owned, own_rows), bf16),
                 pltpu.VMEM((members, owned, own_rows), bf16),
+                pltpu.VMEM((2, 128, 128), f32),
+                pltpu.VMEM((128, 128), f32),
                 dma((3 + 2 * ADJ_PARTS,)),
                 dma((2, chain * PARTS)),
                 dma((chain * PARTS,)),
@@ -753,20 +781,21 @@
                 dma((members,)),
             ],
             compiler_params=pltpu.CompilerParams(
-                collective_id=0, has_side_effects=True, vmem_limit_bytes=48 * 1024 * 1024
+                collective_id=0, has_side_effects=True, vmem_limit_bytes=63 * 1024 * 1024
             ),
             name="fused_section",
         )(
             section_input,
-            conv_taps,
-            dilation_level[:, None],
-            pointwise_matrix,
+            conv_taps.T,
+            dilation_level[None, :],
+            pointwise_matrix.T,
             head_weight,
-            pred_error,
-            tail_mask,
+            pred_error.T,
+            tail_mask.T,
             track_scale[None, :],
         )
     )
+    return input_grad, taps_grad.T
 
 
 def local_or_fused(sizes, *args):
@@ -779,7 +808,11 @@
         and head_weight.shape[0] % (2 * PARTS * 16) == 0
         and section_input.shape[0] % (seq * 16) == 0
         and section_input.shape[1] % 128 == 0
-        and pred_error.shape[0] % (ADJ_PARTS * 16) == 0
+        and pred_error.shape[1] % 16 == 0
+        and pred_error.shape[1] >= 128 * ADJ_PARTS
+        and args[3].shape[1] % 32 == 0
+        and section_input.shape[0] % 256 == 0
+        and section_input.shape[0] // seq <= 128
         and head_weight.shape[0] % (section_input.shape[0] // seq) == 0
     )
     if fits:

time: 109 us -> 97.3 us (0.89)
  local copies, waits for them, and re-layouts: 11.8 us -> 4.31 us
  Pallas kernels: 95.9 us -> 92 us
    unnamed x11 -> x2, local copies, waits for them, and re-layouts: 9.67 us -> 3 us
    pallas_call x1, Pallas kernels: 95.9 us -> 92 us  [fused(): pl.pallas_call(functools.partial(fused_kernel, chain), out_shape=(jax.Sha...]
where the time goes in v2:
time: 97.3 us; the launch traced here: 97 us
  Pallas kernels  92 us (95%)
  local copies, waits for them, and re-layouts  4.31 us (4%)
    pallas_call x1, Pallas kernels, fused(): pl.pallas_call(functools.partial(fused_kernel, chain), out_shape=(jax.Sha...  92 us
    unnamed x2, local copies, waits for them, and re-layouts  3 us

profile of v2, /device:TPU:0, one launch (start us, length us, event | category | flops | bytes accessed | tf_op | source)
XLA Modules:
  0.0 97.0 jit_solution(2230616292333249584)
XLA Ops:
  0.6 1.3 %broadcast_in_dim.7.scale = f32[1,2656]{1,0:T(1,128)} reshape(f32[2656]{0:T(1024)} %param.15) | data formatting | bytes 21248 | tf_op jit(solution)/shard_map/broadcast_in_dim | solution.py:795
  1.9 92.0 %fused_section.1 = (bf16[768,256]{1,0:T(8,128)(2,1)}, f32[3,96]{1,0:T(4,128)}) custom-call(bf16[768,256]{1,0:T(8,128)(2,1)} %sec.1, f32[3,96]{1,0:T(4,128)} %bitcast.9, s32[1,96]{1,0:T(1,128)} %bitcast.11, bf16[192,768]{1,0:T(8,128)(2,1)} %bitcast.8, bf16[192,2656]{1,0:T(8,128)(2,1)} %hw.1, bf16[2656,256]{1,0:T(8,128)(2,1)} %bitcast.7, s32[2656,256]{1,0:T(8,128)} %bitcast.6, ...), custom_call_target="tpu_custom_call" | custom-call | tf_op jit(solution)/shard_map/fused_section/pallas_call | solution.py:734
  94.0 1.8 %copy.12 = bf16[768,256]{1,0:T(8,128)(2,1)} copy(bf16[768,256]{1,0:T(8,128)(2,1)} %get-tuple-element.8) | data formatting | bytes 786432
  95.7 1.2 %copy.13 = f32[96,3]{0,1:T(4,128)} copy(f32[96,3]{0,1:T(4,128)} %bitcast.10) | data formatting | bytes 2304

commit v3 on v2

--- a/solution.py
+++ b/solution.py
@@ -118,8 +118,9 @@
 
 MESH = pl.DeviceIdType.MESH
 CROSS = 2
-PARTS = 3
+PARTS = 6
 ADJ_PARTS = 4
+BACK_PARTS = 3
 
 
 def fused_kernel(
@@ -147,7 +148,8 @@
     hr,
     xr,
     xp,
-    hf,
+    hx,
+    hq,
     cb,
     rb,
     cols,
@@ -169,6 +171,8 @@
     o_recv,
     x_send,
     x_recv,
+    c_send,
+    c_recv,
     h_send,
     h_recv,
     r_send,
@@ -315,7 +319,7 @@
 
         def fill(begin, count):
             rows = pl.ds(begin, count)
-            line = scale[:, rows]
+            line = scale[rows].reshape(1, count)
             if count < 128:
                 line = jnp.concatenate([line, jnp.zeros((1, 128 - count), jnp.float32)], axis=1)
             column = jnp.transpose(jnp.broadcast_to(line, (128, 128)))[:count]
@@ -355,7 +359,6 @@
         x_copy(peer(k), s).start()
         return carry
 
-    lax.fori_loop(1, members, x_start, 0)
 
     below = z
     above = chain - 1 - z
@@ -463,6 +466,7 @@
         return carry
 
     lax.fori_loop(1, steps + 1, p_relay, 0)
+    lax.fori_loop(1, members, x_start, 0)
     last = order(steps)
     wait_swaps(last)
     head_dot(last, x)
@@ -509,13 +513,23 @@
     def h_rows(to):
         return pl.ds(pl.multiple_of(to * owned, 16), owned)
 
+    def c_copy(level_z):
+        return pltpu.make_async_remote_copy(
+            src_ref=hs.at[h_rows(level_z * CROSS + 1 - x), :],
+            dst_ref=hx.at[level_z],
+            send_sem=c_send.at[level_z],
+            recv_sem=c_recv.at[level_z],
+            device_id=across,
+            device_id_type=MESH,
+        )
+
     def h_copy(to, frm):
         return pltpu.make_async_remote_copy(
-            src_ref=hs.at[h_rows(to), :],
+            src_ref=hq.at[to],
             dst_ref=hr.at[frm],
             send_sem=h_send.at[to],
             recv_sem=h_recv.at[frm],
-            device_id=(g, to, t),
+            device_id=(g, to * CROSS + x, t),
             device_id_type=MESH,
         )
 
@@ -534,17 +548,25 @@
                 preferred_element_type=jnp.float32,
             )
         hs[lanes, :] = total.astype(jnp.bfloat16)
-        for u in range(group):
-            to = n * group + u
-
-            @pl.when(to != s)
-            def _():
-                h_copy(to, s).start()
-
+        for u in range(group // CROSS):
+            c_copy(n * (group // CROSS) + u).start()
         return carry
 
     lax.fori_loop(0, 2, h_step, 0)
-    hr[s] = hs[h_rows(s), :]
+
+    def h_sum(to):
+        c_copy(to).wait_recv()
+        mine = hs[h_rows(to * CROSS + x), :].astype(jnp.float32)
+        return (mine + hx[to].astype(jnp.float32)).astype(jnp.bfloat16)
+
+    def h_pass(k, carry):
+        to = order(steps - k)
+        hq[to] = h_sum(to)
+        h_copy(to, z).start()
+        return carry
+
+    lax.fori_loop(0, steps, h_pass, 0)
+    hr[z] = h_sum(z)
 
     own_x.wait()
 
@@ -556,15 +578,6 @@
     for m in range(members):
         xp[:, m * own_rows : (m + 1) * own_rows] = xr[m].astype(jnp.float32)
     xp[:, length:] = jnp.zeros((owned, span), jnp.float32)
-
-    def h_wait(k, carry):
-        h_copy(s, peer(k)).wait_recv()
-        return carry
-
-    lax.fori_loop(1, members, h_wait, 0)
-    for m in range(chain):
-        both = hr[CROSS * m].astype(jnp.float32) + hr[CROSS * m + 1].astype(jnp.float32)
-        hf[:, m * pair_rows : (m + 1) * pair_rows] = both.astype(jnp.bfloat16)
 
     columns = cols.at[1]
     cols[0] = jnp.zeros((128, 128), jnp.float32)
@@ -572,6 +585,12 @@
     cols[0, 3:4, 0:owned] = level[...].astype(jnp.float32)
     cols[1] = jnp.transpose(cols[0])
     sums[...] = jnp.zeros((128, 128), jnp.float32)
+
+    def h_wait(j, carry):
+        h_copy(z, order(j)).wait_recv()
+        return carry
+
+    lax.fori_loop(1, steps + 1, h_wait, 0)
 
     padded = length + span
     norm = 1.0 / math.sqrt(length)
@@ -594,7 +613,8 @@
         plus = pick(wide, 1)
         center = wide[:, :length]
         pre_act = tap[:, 0:1] * minus + tap[:, 1:2] * center + tap[:, 2:3] * plus
-        pre_grad = hf[rows, :].astype(jnp.float32) * gelu_slope(pre_act)
+        hidden = jnp.concatenate([hr[m, rows, :] for m in range(chain)], axis=1)
+        pre_grad = hidden.astype(jnp.float32) * gelu_slope(pre_act)
         sums[rows, 0:1] = jnp.sum(pre_grad * minus, axis=1, keepdims=True) * norm
         sums[rows, 1:2] = jnp.sum(pre_grad * center, axis=1, keepdims=True) * norm
         sums[rows, 2:3] = jnp.sum(pre_grad * plus, axis=1, keepdims=True) * norm
@@ -608,29 +628,37 @@
             cb[m, rows, :] = part[:, m * own_rows : (m + 1) * own_rows]
         return carry
 
-    lax.fori_loop(0, owned // 16, conv_rows, 0)
-
-    def r_copy(to, frm):
-        return pltpu.make_async_remote_copy(
-            src_ref=cb.at[to],
-            dst_ref=rb.at[frm],
-            send_sem=r_send.at[to],
-            recv_sem=r_recv.at[frm],
+    back = owned // BACK_PARTS
+
+    def r_copy(to, frm, c):
+        rows = pl.ds(pl.multiple_of(c * back, 16), back)
+        return pltpu.make_async_remote_copy(
+            src_ref=cb.at[to, rows, :],
+            dst_ref=rb.at[frm, rows, :],
+            send_sem=r_send.at[to, c],
+            recv_sem=r_recv.at[frm, c],
             device_id=(g, to, t),
             device_id_type=MESH,
         )
 
-    def r_start(k, carry):
-        r_copy(peer(k), s).start()
-        return carry
-
-    lax.fori_loop(1, members, r_start, 0)
+    def conv_part(c, carry):
+        lax.fori_loop(c * (back // 16), (c + 1) * (back // 16), conv_rows, 0)
+
+        def r_start(k, inner):
+            r_copy(peer(k), s, c).start()
+            return inner
+
+        lax.fori_loop(1, members, r_start, 0)
+        return carry
+
+    lax.fori_loop(0, BACK_PARTS, conv_part, 0)
     rb[s] = cb[s]
     for q in range(blocks_kept):
         o_copy(q).wait_recv()
 
     def r_wait(k, carry):
-        r_copy(s, peer(k)).wait_recv()
+        for c in range(BACK_PARTS):
+            r_copy(s, peer(k), c).wait_recv()
         return carry
 
     lax.fori_loop(1, members, r_wait, 0)
@@ -689,6 +717,12 @@
 
         for xs in range(CROSS):
             g_copy(shard, xs).wait_send()
+        c_copy(shard).wait_send()
+
+        @pl.when(shard != z)
+        def _():
+            h_copy(shard, z).wait_send()
+
         return carry
 
     lax.fori_loop(0, chain, w_done, 0)
@@ -700,8 +734,8 @@
 
     def done(k, carry):
         x_copy(peer(k), s).wait_send()
-        h_copy(peer(k), s).wait_send()
-        r_copy(peer(k), s).wait_send()
+        for c in range(BACK_PARTS):
+            r_copy(peer(k), s, c).wait_send()
         return carry
 
     lax.fori_loop(1, members, done, 0)
@@ -750,10 +784,11 @@
                 pltpu.VMEM((chain * head_rows, pair_rows), bf16),
                 pltpu.VMEM((chain // 2, head_rows, own_rows), bf16),
                 pltpu.VMEM((own, pair_rows), bf16),
-                pltpu.VMEM((members, owned, pair_rows), bf16),
+                pltpu.VMEM((chain, owned, pair_rows), bf16),
                 pltpu.VMEM((members, owned, own_rows), bf16),
                 pltpu.VMEM((owned, length + span), f32),
-                pltpu.VMEM((owned, length), bf16),
+                pltpu.VMEM((chain, owned, pair_rows), bf16),
+                pltpu.VMEM((chain, owned, pair_rows), bf16),
                 pltpu.VMEM((members, owned, own_rows), bf16),
                 pltpu.VMEM((members, owned, own_rows), bf16),
                 pltpu.VMEM((2, 128, 128), f32),
@@ -775,10 +810,12 @@
                 dma((chain // 2,)),
                 dma((members,)),
                 dma((members,)),
-                dma((members,)),
-                dma((members,)),
-                dma((members,)),
-                dma((members,)),
+                dma((chain,)),
+                dma((chain,)),
+                dma((chain,)),
+                dma((chain,)),
+                dma((members, BACK_PARTS)),
+                dma((members, BACK_PARTS)),
             ],
             compiler_params=pltpu.CompilerParams(
                 collective_id=0, has_side_effects=True, vmem_limit_bytes=63 * 1024 * 1024
@@ -792,7 +829,7 @@
             head_weight,
             pred_error.T,
             tail_mask.T,
-            track_scale[None, :],
+            track_scale,
         )
     )
     return input_grad, taps_grad.T
@@ -813,6 +850,7 @@
         and args[3].shape[1] % 32 == 0
         and section_input.shape[0] % 256 == 0
         and section_input.shape[0] // seq <= 128
+        and section_input.shape[0] // seq % (BACK_PARTS * 16) == 0
         and head_weight.shape[0] % (section_input.shape[0] // seq) == 0
     )
     if fits:

time: 97.3 us -> 91.9 us (0.945)
  Pallas kernels: 92 us -> 88 us
  local copies, waits for them, and re-layouts: 4.31 us -> 3 us
    pallas_call x1, Pallas kernels: 92 us -> 88 us  [fused(): pl.pallas_call(functools.partial(fused_kernel, chain), out_shape=(jax.Sha...]
    broadcast_in_dim x1 -> x0, local copies, waits for them, and re-layouts: 1.31 us -> none  [fused(): track_scale[None, :]]
where the time goes in v3:
time: 91.9 us; the launch traced here: 91.7 us
  Pallas kernels  88 us (96%)
  local copies, waits for them, and re-layouts  3 us (3%)
    pallas_call x1, Pallas kernels, fused(): pl.pallas_call(functools.partial(fused_kernel, chain), out_shape=(jax.Sha...  88 us
    unnamed x2, local copies, waits for them, and re-layouts  3 us

profile of v3, /device:TPU:0, one launch (start us, length us, event | category | flops | bytes accessed | tf_op | source)
XLA Modules:
  0.0 91.7 jit_solution(15102182248770017593)
XLA Ops:
  0.6 88.0 %fused_section.1 = (bf16[768,256]{1,0:T(8,128)(2,1)}, f32[3,96]{1,0:T(4,128)}) custom-call(bf16[768,256]{1,0:T(8,128)(2,1)} %sec.1, f32[3,96]{1,0:T(4,128)} %bitcast.9, s32[1,96]{1,0:T(1,128)} %bitcast.11, bf16[192,768]{1,0:T(8,128)(2,1)} %bitcast.8, bf16[192,2656]{1,0:T(8,128)(2,1)} %hw.1, bf16[2656,256]{1,0:T(8,128)(2,1)} %bitcast.7, s32[2656,256]{1,0:T(8,128)} %bitcast.6, ...), custom_call_target="tpu_custom_call" | custom-call | tf_op jit(solution)/shard_map/fused_section/pallas_call | solution.py:768
  88.7 1.8 %copy.12 = bf16[768,256]{1,0:T(8,128)(2,1)} copy(bf16[768,256]{1,0:T(8,128)(2,1)} %get-tuple-element.8) | data formatting | bytes 786432
  90.4 1.2 %copy.13 = f32[96,3]{0,1:T(4,128)} copy(f32[96,3]{0,1:T(4,128)} %bitcast.10) | data formatting | bytes 2304

commit v4 on v3

--- a/solution.py
+++ b/solution.py
@@ -121,6 +121,7 @@
 PARTS = 6
 ADJ_PARTS = 4
 BACK_PARTS = 3
+P_PARTS = 3
 
 
 def fused_kernel(
@@ -262,23 +263,30 @@
             device_id_type=MESH,
         )
 
-    def p_hop(shard, src, toward, direction):
+    p_piece = phalf // P_PARTS
+
+    def p_rows(c, which):
+        return pl.ds(pl.multiple_of(which * phalf + c * p_piece, 16), p_piece)
+
+    def p_hop(shard, c, src, toward, direction):
+        slot = shard * P_PARTS + c
         return pltpu.make_async_remote_copy(
             src_ref=src,
-            dst_ref=pb.at[shard, pl.ds(pl.multiple_of(g * phalf, 16), phalf), :],
-            send_sem=p_send.at[direction, shard],
-            recv_sem=p_recv.at[shard],
+            dst_ref=pb.at[shard, p_rows(c, g), :],
+            send_sem=p_send.at[direction, slot],
+            recv_sem=p_recv.at[slot],
             device_id=(g, toward * CROSS + x, t),
             device_id_type=MESH,
         )
 
-    def p_swap(shard, which):
-        block = pb.at[shard, pl.ds(pl.multiple_of(which * phalf, 16), phalf), :]
+    def p_swap(shard, c, which):
+        slot = shard * P_PARTS + c
+        block = pb.at[shard, p_rows(c, which), :]
         return pltpu.make_async_remote_copy(
             src_ref=block,
             dst_ref=block,
-            send_sem=py_send.at[shard],
-            recv_sem=py_recv.at[shard],
+            send_sem=py_send.at[slot],
+            recv_sem=py_recv.at[slot],
             device_id=twin,
             device_id_type=MESH,
         )
@@ -289,7 +297,6 @@
     def own_piece(c):
         return hw.at[pl.ds(pl.multiple_of(g * half + c * piece, 16), piece), :]
 
-    own_phalf = pw.at[pl.ds(pl.multiple_of(g * phalf, 16), phalf), :]
 
     @pl.when(has_up)
     def _():
@@ -339,11 +346,13 @@
 
     @pl.when(has_up)
     def _():
-        p_hop(z, own_phalf, z + 1, 0).start()
+        for c in range(P_PARTS):
+            p_hop(z, c, pw.at[p_rows(c, g), :], z + 1, 0).start()
 
     @pl.when(has_down)
     def _():
-        p_hop(z, own_phalf, z - 1, 1).start()
+        for c in range(P_PARTS):
+            p_hop(z, c, pw.at[p_rows(c, g), :], z - 1, 1).start()
 
     def x_copy(to, frm):
         return pltpu.make_async_remote_copy(
@@ -449,28 +458,30 @@
 
     lax.fori_loop(0, steps, late, 0)
 
-    def p_relay(j, carry):
-        shard = order(j)
-        block = pb.at[shard, pl.ds(pl.multiple_of(g * phalf, 16), phalf), :]
-        p_hop(shard, block, z, 0).wait_recv()
+    def p_relay(e, carry):
+        shard = order(e // P_PARTS + 1)
+        c = e % P_PARTS
+        block = pb.at[shard, p_rows(c, g), :]
+        p_hop(shard, c, block, z, 0).wait_recv()
 
         @pl.when((shard < z) & has_up)
         def _():
-            p_hop(shard, block, z + 1, 0).start()
+            p_hop(shard, c, block, z + 1, 0).start()
 
         @pl.when((shard > z) & has_down)
         def _():
-            p_hop(shard, block, z - 1, 1).start()
-
-        p_swap(shard, g).start()
-        return carry
-
-    lax.fori_loop(1, steps + 1, p_relay, 0)
-    lax.fori_loop(1, members, x_start, 0)
+            p_hop(shard, c, block, z - 1, 1).start()
+
+        p_swap(shard, c, g).start()
+        return carry
+
+    lax.fori_loop(0, (steps - 1) * P_PARTS, p_relay, 0)
     last = order(steps)
     wait_swaps(last)
     head_dot(last, x)
     head_dot(last, 1 - x)
+    lax.fori_loop(1, members, x_start, 0)
+    lax.fori_loop((steps - 1) * P_PARTS, steps * P_PARTS, p_relay, 0)
 
     def core_sum(j, carry):
         shard = jnp.where(j == 0, z, order(jnp.maximum(j, 1)))
@@ -505,7 +516,8 @@
     own_p.wait()
 
     def p_wait(j, carry):
-        p_swap(order(j), 1 - g).wait_recv()
+        for c in range(P_PARTS):
+            p_swap(order(j), c, 1 - g).wait_recv()
         return carry
 
     lax.fori_loop(1, steps + 1, p_wait, 0)
@@ -701,19 +713,20 @@
             return inner
 
         lax.fori_loop(0, PARTS, one, 0)
-        pblock = pb.at[shard, pl.ds(pl.multiple_of(g * phalf, 16), phalf), :]
-
-        @pl.when((shard <= z) & has_up)
-        def _():
-            p_hop(shard, pblock, z, 0).wait_send()
-
-        @pl.when((shard >= z) & has_down)
-        def _():
-            p_hop(shard, pblock, z, 1).wait_send()
-
-        @pl.when(shard != z)
-        def _():
-            p_swap(shard, g).wait_send()
+        for c in range(P_PARTS):
+            pblock = pb.at[shard, p_rows(c, g), :]
+
+            @pl.when((shard <= z) & has_up)
+            def _():
+                p_hop(shard, c, pblock, z, 0).wait_send()
+
+            @pl.when((shard >= z) & has_down)
+            def _():
+                p_hop(shard, c, pblock, z, 1).wait_send()
+
+            @pl.when(shard != z)
+            def _():
+                p_swap(shard, c, g).wait_send()
 
         for xs in range(CROSS):
             g_copy(shard, xs).wait_send()
@@ -798,10 +811,10 @@
                 dma((chain * PARTS,)),
                 dma((chain * PARTS,)),
                 dma((chain * PARTS,)),
-                dma((2, chain)),
-                dma((chain,)),
-                dma((chain,)),
-                dma((chain,)),
+                dma((2, chain * P_PARTS)),
+                dma((chain * P_PARTS,)),
+                dma((chain * P_PARTS,)),
+                dma((chain * P_PARTS,)),
                 dma((ADJ_PARTS,)),
                 dma((ADJ_PARTS,)),
                 dma((chain, CROSS)),
@@ -847,7 +860,7 @@
         and section_input.shape[1] % 128 == 0
         and pred_error.shape[1] % 16 == 0
         and pred_error.shape[1] >= 128 * ADJ_PARTS
-        and args[3].shape[1] % 32 == 0
+        and args[3].shape[1] % (2 * P_PARTS * 16) == 0
         and section_input.shape[0] % 256 == 0
         and section_input.shape[0] // seq <= 128
         and section_input.shape[0] // seq % (BACK_PARTS * 16) == 0

time: 91.9 us -> 90.8 us (0.988)
  Pallas kernels: 88 us -> 86.9 us
    pallas_call x1, Pallas kernels: 88 us -> 86.9 us  [fused(): pl.pallas_call(functools.partial(fused_kernel, chain), out_shape=(jax.Sha...]
where the time goes in v4:
time: 90.8 us; the launch traced here: 90.6 us
  Pallas kernels  86.9 us (96%)
  local copies, waits for them, and re-layouts  3 us (3%)
    pallas_call x1, Pallas kernels, fused(): pl.pallas_call(functools.partial(fused_kernel, chain), out_shape=(jax.Sha...  86.9 us
    unnamed x2, local copies, waits for them, and re-layouts  3 us

profile of v4, /device:TPU:0, one launch (start us, length us, event | category | flops | bytes accessed | tf_op | source)
XLA Modules:
  0.0 90.6 jit_solution(6710313500105732571)
XLA Ops:
  0.6 86.9 %fused_section.1 = (bf16[768,256]{1,0:T(8,128)(2,1)}, f32[3,96]{1,0:T(4,128)}) custom-call(bf16[768,256]{1,0:T(8,128)(2,1)} %sec.1, f32[3,96]{1,0:T(4,128)} %bitcast.9, s32[1,96]{1,0:T(1,128)} %bitcast.11, bf16[192,768]{1,0:T(8,128)(2,1)} %bitcast.8, bf16[192,2656]{1,0:T(8,128)(2,1)} %hw.1, bf16[2656,256]{1,0:T(8,128)(2,1)} %bitcast.7, s32[2656,256]{1,0:T(8,128)} %bitcast.6, ...), custom_call_target="tpu_custom_call" | custom-call | tf_op jit(solution)/shard_map/fused_section/pallas_call | solution.py:781
  87.6 1.8 %copy.12 = bf16[768,256]{1,0:T(8,128)(2,1)} copy(bf16[768,256]{1,0:T(8,128)(2,1)} %get-tuple-element.8) | data formatting | bytes 786432
  89.3 1.2 %copy.13 = f32[96,3]{0,1:T(4,128)} copy(f32[96,3]{0,1:T(4,128)} %bitcast.10) | data formatting | bytes 2304

commit v5 on v4

--- a/solution.py
+++ b/solution.py
@@ -510,9 +510,6 @@
             device_id_type=MESH,
         )
 
-    for q in range(blocks_kept):
-        o_copy(q).start()
-
     own_p.wait()
 
     def p_wait(j, carry):
@@ -565,6 +562,9 @@
         return carry
 
     lax.fori_loop(0, 2, h_step, 0)
+
+    for q in range(blocks_kept):
+        o_copy(q).start()
 
     def h_sum(to):
         c_copy(to).wait_recv()

time: 90.8 us -> 89.4 us (0.985)
  Pallas kernels: 86.9 us -> 85.5 us
    pallas_call x1, Pallas kernels: 86.9 us -> 85.5 us  [fused(): pl.pallas_call(functools.partial(fused_kernel, chain), out_shape=(jax.Sha...]
where the time goes in v5:
time: 89.4 us; the launch traced here: 89.2 us
  Pallas kernels  85.5 us (96%)
  local copies, waits for them, and re-layouts  3 us (3%)
    pallas_call x1, Pallas kernels, fused(): pl.pallas_call(functools.partial(fused_kernel, chain), out_shape=(jax.Sha...  85.5 us
    unnamed x2, local copies, waits for them, and re-layouts  3 us

profile of v5, /device:TPU:0, one launch (start us, length us, event | category | flops | bytes accessed | tf_op | source)
XLA Modules:
  0.0 89.2 jit_solution(3964753941671710067)
XLA Ops:
  0.6 85.5 %fused_section.1 = (bf16[768,256]{1,0:T(8,128)(2,1)}, f32[3,96]{1,0:T(4,128)}) custom-call(bf16[768,256]{1,0:T(8,128)(2,1)} %sec.1, f32[3,96]{1,0:T(4,128)} %bitcast.9, s32[1,96]{1,0:T(1,128)} %bitcast.11, bf16[192,768]{1,0:T(8,128)(2,1)} %bitcast.8, bf16[192,2656]{1,0:T(8,128)(2,1)} %hw.1, bf16[2656,256]{1,0:T(8,128)(2,1)} %bitcast.7, s32[2656,256]{1,0:T(8,128)} %bitcast.6, ...), custom_call_target="tpu_custom_call" | custom-call | tf_op jit(solution)/shard_map/fused_section/pallas_call | solution.py:781
  86.2 1.8 %copy.12 = bf16[768,256]{1,0:T(8,128)(2,1)} copy(bf16[768,256]{1,0:T(8,128)(2,1)} %get-tuple-element.8) | data formatting | bytes 786432
  87.9 1.2 %copy.13 = f32[96,3]{0,1:T(4,128)} copy(f32[96,3]{0,1:T(4,128)} %bitcast.10) | data formatting | bytes 2304
